TPU v7x, 32 devices: a whole 2x2x4 slice. The times are simulated.
32 devices in a mesh: space: 16 (over z, y, x), phase: 2 (over core).
Axes of the slice: x: 2, y: 2, z: 4, core: 2. Of those that a mesh axis runs over, the one named last changes fastest.
Arguments:
- particle_cell: int32 [2, 1024, 128], P('phase', 'space'), may hold values from 0 to 63
- block_count: int32 [2, 1024], P('phase', 'space'), may hold values from 1 to 128, as said below
- particle_frac: float32 [2, 3, 1024, 128], P('phase', None, 'space'), may hold values from 0 to 1
- particle_vel: float32 [2, 3, 1024, 128], P('phase', None, 'space'), may hold values from -2.5 to 2.5
- particle_mass: float32 [2, 1024, 128], P('phase', 'space'), may hold values from 0.5 to 2
- particle_stress: float32 [2, 1024, 128], P('phase', 'space'), may hold values from -6 to 6
- drag_coef: float32 [64, 8, 128], P('space'), may hold values from 0.2 to 5
Outputs:
- frac_out: float32 [2, 3, 1024, 128], P('phase', None, 'space')
- vel_out: float32 [2, 3, 1024, 128], P('phase', None, 'space')
- stress_out: float32 [2, 1024, 128], P('phase', 'space')
Inputs may be any that keep to these rules, and one draw needn't show every extreme that they name: `particle_cell`: the cell of a slot within its block of 4 x 4 x 4 cells, numbered 16 a + 4 b + c for the offsets a, b, c along the first, second and third dimension. `block_count`: slots 0 to count - 1 of a block hold particles, the others are empty; among the blocks b with the same b // 64 in a phase, one has all 128 slots live.
All inputs are finite; a program needn't handle non-finite values.
Results may differ from a plain program's by a relative error of at most 0.0003.
Values sent between devices are 32-bit elements; how exact they have to be, the bound alone decides.
No kernel may reach another device: no remote copies, remote signals or barrier semaphores. Data moves between devices by JAX's collectives and lax.ppermute only.
A program may use at most 64 MiB of HBM per device.

v0:
```python
import functools

import jax
import jax.numpy as jnp
from jax import lax
from jax.experimental import pallas as pl
from jax.experimental.pallas import tpu as pltpu
from jax.sharding import PartitionSpec as P


time_step = 0.05
gravity = 1.0
bulk_modulus = 4.0
mass_floor = 0.25
slip_floor = 0.25

F32 = jnp.float32
BF16 = jnp.bfloat16

WX, YAT, WY, ZAT, WZ, DZ = 0, 6, 7, 10, 11, 14
CHANNEL = 17
PLANES = 22
XC, YC, LIVE = 0, 1, 2

GROUP = 4
WINDOW = 24
EDGE = 1
CHANNELS = 5


def spline(frac):
    r = frac - 0.5
    low, high = 0.5 - r, 0.5 + r
    w = (0.5 * low * low, 0.75 - r * r, 0.5 * high * high)
    d = ((-1.0 - r) * w[0], -r * w[1], (1.0 - r) * w[2])
    return w, d


def place(where_at, first, values):
    k = where_at - first
    out = jnp.where(k == 2.0, values[2], 0.0)
    out = jnp.where(k == 1.0, values[1], out)
    return jnp.where(k == 0.0, values[0], out)


def halves(value):
    high = value.astype(BF16)
    return high, (value - high.astype(F32)).astype(BF16)


def prepare(cell, frac, planes, kept, mass, vel, stress, nby, nbz):
    wx, _ = spline(frac[0])
    wy, _ = spline(frac[1])
    wz, dz = spline(frac[2])
    at_x = (cell >> 4).astype(F32)
    at_y = ((cell >> 2) & 3).astype(F32)
    block = lax.broadcasted_iota(jnp.int32, cell.shape, 0)
    at_y = at_y + 4.0 * sum((block >= nbz * k).astype(F32) for k in range(1, nby))
    planes[YAT] = at_y
    planes[ZAT] = (cell & 3).astype(F32)
    for t in range(3):
        planes[WY + t] = wy[t]
        planes[WZ + t] = wz[t]
        planes[DZ + t] = dz[t]
    for x in range(6):
        planes[WX + x] = place(float(x), at_x, wx)
    position = (at_x + (frac[0] - 2.0), at_y + (frac[1] - 2.0 * nby))
    kept[XC] = position[0]
    kept[YC] = position[1]
    scaled = (4.0 * time_step) * stress
    planes[CHANNEL] = mass
    planes[CHANNEL + 1] = mass * vel[0] - scaled * position[0]
    planes[CHANNEL + 2] = mass * vel[1] - scaled * position[1]
    planes[CHANNEL + 3] = mass * vel[2]
    planes[CHANNEL + 4] = scaled


def z_rows(q):
    return 4 * q // 8 * 8, (4 * q + 5) // 8 * 8 + 8


def side_by_side(ref, rows):
    return jnp.concatenate([ref[row] for row in rows], axis=1)


def block_row(h, b, nbz):
    return b // GROUP * nbz + h * GROUP + b % GROUP


def deposit(planes, tiles, factors, right, sums, out, nby, nbz):
    sums[...] = jnp.zeros_like(sums)
    blocks = nby * GROUP

    def group(h, carry):
        for b in range(blocks):
            row, q = block_row(h, b, nbz), b % GROUP
            get = lambda k: planes[k, pl.ds(row, 8, stride=0), :]
            at = lax.broadcasted_iota(jnp.int32, (8, 128), 0).astype(F32)
            wy = place(at, get(YAT) - 1.0, [get(WY + t) for t in range(3)])
            for x in range(0, 6, 2):
                high, low = halves(jnp.concatenate([get(WX + x) * wy, get(WX + x + 1) * wy], axis=0))
                tiles[row, 8 * x : 8 * x + 16] = high
                tiles[row, 48 + 8 * x : 64 + 8 * x] = low
            first, last = z_rows(q)
            steps = (last - first) // 8
            get = lambda k: jnp.concatenate([planes[k, pl.ds(row, 8, stride=0), :]] * steps, axis=0)
            at = lax.broadcasted_iota(jnp.int32, (last - first, 128), 0).astype(F32)
            start = get(ZAT) + float(4 * q - first)
            wz = place(at, start, [get(WZ + t) for t in range(3)])
            dz = place(at, start, [get(DZ + t) for t in range(3)])
            factors[row, 0, 0 : last - first] = wz
            factors[row, 1, 0 : last - first] = dz
            parts = [get(CHANNEL + c) * wz for c in range(CHANNELS)]
            parts[3] = parts[3] + get(CHANNEL + 4) * dz
            zeros = lambda n: [jnp.zeros((n, 128), F32)] if n else []
            high = [part.astype(BF16).astype(F32) for part in parts]
            low = [part - h for part, h in zip(parts, high)]
            for at, values in ((0, high), (128, low)):
                stack = []
                for value in values:
                    stack += zeros(first) + [value] + zeros(WINDOW - last)
                stack += zeros(128 - CHANNELS * WINDOW)
                right[b, at : at + 128] = jnp.concatenate(stack, axis=0).astype(BF16)
        a = side_by_side(tiles, [block_row(h, b, nbz) for b in range(blocks)])
        o = lax.dot_general(a, side_by_side(right, range(blocks)), (((1,), (1,)), ((), ())),
                            preferred_element_type=F32)
        o = o[0:48] + o[48:96]
        o = o[:, 0:128] + o[:, 128:256]
        z = lax.broadcasted_iota(jnp.int32, o.shape, 1) - (4 * GROUP * h - EDGE)
        inside = (z >= 0) & (z < WINDOW)
        for c in range(CHANNELS):
            moved = pltpu.roll(o, lax.rem(4 * GROUP * h + (128 - EDGE + 128 - WINDOW * c), 128), 1)
            sums[c] += jnp.where(inside, moved, 0.0)
        return carry

    lax.fori_loop(0, nbz // GROUP, group, 0, unroll=True)
    shape = out.shape[1:]
    x = lax.broadcasted_iota(jnp.int32, shape, 0).astype(F32) - 2.5
    y = lax.broadcasted_iota(jnp.int32, shape, 1).astype(F32) + (0.5 - 2.0 * nby)
    mass, mx, my, mz, stress = (sums[c].reshape(shape) for c in range(CHANNELS))
    out[0] = mass
    out[1] = mx + x * stress
    out[2] = my + y * stress
    out[3] = mz


def gather(vel, tiles, factors, turned, sampled, nby, nbz):
    blocks = nby * GROUP
    shape = vel[0].shape
    x = lax.broadcasted_iota(jnp.int32, shape, 0).astype(F32) - 2.5
    y = lax.broadcasted_iota(jnp.int32, shape, 1).astype(F32) + (0.5 - 2.0 * nby)
    for c, v in enumerate((vel[0], vel[1], vel[2], x * vel[0] + y * vel[1])):
        v = v.reshape(48, 128)
        high = v.astype(BF16).astype(F32)
        v = jnp.concatenate([high, v - high, jnp.zeros((32, 128), F32)], axis=0)
        turned[c, 0:8] = jnp.zeros((8, 128), F32)
        turned[c, 128:152] = jnp.zeros((24, 128), F32)
        turned[c, EDGE : EDGE + 128] = v.T
    pad = jnp.zeros((32, 128), F32).astype(BF16)

    def group(h, carry):
        at = pl.multiple_of(4 * GROUP * h, 8)
        v = jnp.concatenate([turned[c, pl.ds(at, WINDOW)] for c in range(4)], axis=0).astype(BF16)
        rows = [block_row(h, b, nbz) for b in range(blocks)]
        stack = []
        for part in (0, 48):
            piece = jnp.concatenate([tiles[row, part : part + 48] for row in rows], axis=1)
            stack += [piece, piece, jnp.concatenate([pad] * blocks, axis=1)]
        t = jnp.dot(jnp.concatenate([v, v], axis=1), jnp.concatenate(stack, axis=0), preferred_element_type=F32)
        for b, row in enumerate(rows):
            first, last = z_rows(b % GROUP)
            w, d = factors[row, 0, 0 : last - first], factors[row, 1, 0 : last - first]
            read = lambda c: t[WINDOW * c + first : WINDOW * c + last, 128 * b : 128 * b + 128]
            vz = read(2)
            for c, value in enumerate((w * read(0), w * read(1), w * vz, w * read(3) + d * vz)):
                sampled[c, pl.ds(row, 1), :] = jnp.sum(value, axis=0, keepdims=True)
        return carry

    lax.fori_loop(0, nbz // GROUP, group, 0, unroll=True)


def node_velocity(fields):
    mass = fields[0]
    inverse = 1.0 / jnp.maximum(mass, mass_floor)
    vel = [fields[k] * inverse for k in (1, 2, 3)]
    lifted = vel[2] - time_step * gravity
    floor = lax.broadcasted_iota(jnp.int32, lifted.shape, 2) == 0
    vel[2] = jnp.where(floor, jnp.maximum(lifted, 0.0), lifted)
    return mass, vel


def dragged(mass, vel, other_mass, other_vel, coef):
    slip = [b - a for a, b in zip(vel, other_vel)]
    rate = coef * jnp.sqrt(slip[0] * slip[0] + slip[1] * slip[1] + slip[2] * slip[2] + slip_floor)
    share = rate / (1.0 + rate) * (other_mass / (mass + other_mass + mass_floor))
    return [a + share * s for a, s in zip(vel, slip)]


class Side:
    def __init__(self):
        place_id = lax.axis_index("space")
        self.even = lax.rem(place_id, 2) == 0
        self.has_left = place_id > 0
        self.has_right = place_id < lax.axis_size("space") - 1

    def arrived(self, first, second, rows):
        first, second = first[rows], second[rows]
        from_left = jnp.where(self.even, second, first)
        from_right = jnp.where(self.even, first, second)
        return jnp.where(self.has_left, from_left, 0.0), jnp.where(self.has_right, from_right, 0.0)

    def layers(self, own, first, second):
        left, right = self.arrived(first, second, slice(0, 8))
        shape = (4, 2) + left.shape[1:]
        own = own[...]
        return jnp.concatenate(
            [own[:, 0:2] + left.reshape(shape), own[:, 2:4], own[:, 4:6] + right.reshape(shape)], axis=1
        )

    def send(self, own, first, second, coef=None):
        toward = jnp.where(self.even, 4, 0)
        for ref, start in ((first, toward), (second, 4 - toward)):
            for c in range(4):
                ref[2 * c : 2 * c + 2] = own[c, pl.ds(start, 2)]
        if coef is not None:
            first[8] = jnp.where(self.even, coef[3], coef[0])
            second[8] = jnp.where(self.even, coef[0], coef[3])

    def keep(self, vel):
        layer = lax.broadcasted_iota(jnp.int32, vel.shape, 0)
        keep = ((layer > 0) | self.has_left) & ((layer < vel.shape[0] - 1) | self.has_right)
        return jnp.where(keep, vel, 0.0)


def live_mask(count, shape):
    square = (shape[0], shape[0])
    same = lax.broadcasted_iota(jnp.int32, square, 0) == lax.broadcasted_iota(jnp.int32, square, 1)
    column = jnp.sum(jnp.where(same, count[...].astype(F32), 0.0), axis=1, keepdims=True)
    return lax.broadcasted_iota(jnp.int32, shape, 1).astype(F32) < column


def advance(sampled, kept, frac_ref, vel_ref, stress_ref):
    live = kept[LIVE] > 0.5
    vel = [sampled[k] for k in range(3)]
    rate = sampled[3] - kept[XC] * vel[0] - kept[YC] * vel[1]
    old = stress_ref[...]
    stress = jnp.where(live, old - (time_step * bulk_modulus * 4.0) * rate, old)
    frac = [jnp.where(live, frac_ref[k] + time_step * vel[k], frac_ref[k]) for k in range(3)]
    vel = [jnp.where(live, vel[k], vel_ref[k]) for k in range(3)]
    return frac, vel, stress


def store_state(state, new_frac, new_vel, new_stress):
    frac, vel, stress = state
    for k in range(3):
        new_frac[k] = frac[k]
        new_vel[k] = vel[k]
    new_stress[...] = stress


def first_kernel(sizes, *refs):
    sources, inputs, rest = refs[:7], refs[7:14], refs[14:]
    kept, tiles, factors, dep, first, second, planes, right, sums, sems = rest
    copies = [pltpu.make_async_copy(a, b, sems.at[k]) for k, (a, b) in enumerate(zip(sources, inputs))]
    for copy in copies:
        copy.start()
    for copy in copies:
        copy.wait()
    cell, count, frac, vel, mass, stress, coef = inputs
    live = live_mask(count, cell.shape)
    kept[LIVE] = jnp.where(live, 1.0, 0.0)
    m = jnp.where(live, mass[...], 0.0)
    s = jnp.where(live, stress[...], 0.0)
    prepare(cell[...], [frac[k] for k in range(3)], planes, kept, m, [vel[k] for k in range(3)], s, *sizes)
    deposit(planes, tiles, factors, right, sums, dep, *sizes)
    Side().send(dep, first, second, coef)


def total_kernel(dep, first, second, fields):
    fields[...] = Side().layers(dep, first, second)


def middle_kernel(sizes, cell, frac, vel, mass, stress, coef, kept, tiles, factors, fields, other, first, second,
                  new_frac, new_vel, new_stress, new_kept, new_tiles, new_factors, dep, new_first, new_second,
                  planes, right, sums, turned, sampled):
    side = Side()
    own_mass, own_vel = node_velocity(fields)
    other_mass, other_vel = node_velocity(other)
    low, high = side.arrived(first, second, slice(8, 9))
    coefs = jnp.concatenate([low, coef[...], high], axis=0)
    nodes = [side.keep(v) for v in dragged(own_mass, own_vel, other_mass, other_vel, coefs)]
    gather(nodes, tiles, factors, turned, sampled, *sizes)
    state = advance(sampled, kept, frac, vel, stress)
    store_state(state, new_frac, new_vel, new_stress)
    new_kept[LIVE] = kept[LIVE]
    live = kept[LIVE] > 0.5
    m = jnp.where(live, mass[...], 0.0)
    s = jnp.where(live, state[2], 0.0)
    prepare(cell[...], state[0], planes, new_kept, m, state[1], s, *sizes)
    deposit(planes, new_tiles, new_factors, right, sums, dep, *sizes)
    side.send(dep, new_first, new_second)


def last_kernel(sizes, frac, vel, stress, kept, tiles, factors, dep, first, second,
                new_frac, new_vel, new_stress, turned, sampled):
    side = Side()
    _, nodes = node_velocity(side.layers(dep, first, second))
    gather([side.keep(v) for v in nodes], tiles, factors, turned, sampled, *sizes)
    store_state(advance(sampled, kept, frac, vel, stress), new_frac, new_vel, new_stress)


def call(kernel, outs, scratch, *args, space=pltpu.VMEM, cost=None, limit=24 << 20):
    spec = pl.BlockSpec(memory_space=space)
    vmem = pl.BlockSpec(memory_space=pltpu.VMEM)
    return pl.pallas_call(
        kernel,
        out_shape=[jax.ShapeDtypeStruct(*(s if isinstance(s[0], tuple) else (s, F32))) for s in outs],
        in_specs=[spec] * len(args),
        out_specs=[vmem] * len(outs),
        scratch_shapes=scratch,
        cost_estimate=cost,
        compiler_params=pltpu.CompilerParams(vmem_limit_bytes=limit),
    )(*args)


def local(particle_cell, block_count, particle_frac, particle_vel, particle_mass, particle_stress, drag_coef):
    cell, count = particle_cell[0], block_count
    frac, vel = particle_frac[0], particle_vel[0]
    mass, stress = particle_mass[0], particle_stress[0]
    layers, ny, nz = drag_coef.shape
    sizes = nby, nbz = ny // 4, nz // 4
    blocks, slots = cell.shape
    places = lax.axis_size("space")

    def matching(start):
        pairs = [(i, i) for i in range(start)]
        for i in range(start, places - 1, 2):
            pairs += [(i, i + 1), (i + 1, i)]
        return pairs + [(i, i) for i in range(len(pairs), places)]

    swap = [(i, i ^ 1) for i in range(lax.axis_size("phase"))]
    particle = (blocks, slots)
    triple = (3,) + particle
    grid = (4, layers + 2, ny, nz)
    saved = [triple, ((blocks, 96, slots), BF16), (blocks, 2, 16, slots)]
    planes = pltpu.VMEM((PLANES,) + particle, F32)
    right = pltpu.VMEM((nby * GROUP, 256, slots), BF16)
    sums = pltpu.VMEM((CHANNELS, (layers + 2) * ny, nz), F32)
    turned = pltpu.VMEM((4, nz + 24, 128), F32)
    sampled = pltpu.VMEM((4,) + particle, F32)

    def exchange(first, second):
        second = lax.ppermute(second, "space", matching(1))
        first = lax.ppermute(first, "space", matching(0))
        return first, second

    inputs = (cell, count, frac, vel, mass, stress, drag_coef)
    sent = (9, ny, nz)
    *loaded, kept, tiles, factors, dep, first, second = call(
        functools.partial(first_kernel, sizes),
        [(a.shape, a.dtype) for a in inputs] + saved + [grid, sent, sent],
        [planes, right, sums, pltpu.SemaphoreType.DMA((7,))],
        *[pltpu.with_memory_space_constraint(a, pltpu.HBM) for a in inputs], space=pltpu.HBM)
    first, second = exchange(first, second)
    fields, = call(total_kernel, [grid], [], dep, first, second)
    other = lax.ppermute(fields, "phase", swap)
    sent = (8, ny, nz)
    frac, vel, stress, kept, tiles, factors, dep, first, second = call(
        functools.partial(middle_kernel, sizes),
        [triple, triple, particle] + saved + [grid, sent, sent],
        [planes, right, sums, turned, sampled],
        loaded[0], *loaded[2:], kept, tiles, factors, fields, other, first, second)
    first, second = exchange(first, second)
    frac, vel, stress = call(
        functools.partial(last_kernel, sizes), [triple, triple, particle], [turned, sampled],
        frac, vel, stress, kept, tiles, factors, dep, first, second)
    return frac[None], vel[None], stress[None]


def solution(mesh):
    in_specs = (
        P("phase", "space", None),
        P("phase", "space"),
        P("phase", None, "space", None),
        P("phase", None, "space", None),
        P("phase", "space", None),
        P("phase", "space", None),
        P("space", None, None),
    )
    out_specs = (
        P("phase", None, "space", None),
        P("phase", None, "space", None),
        P("phase", "space", None),
    )
    return jax.shard_map(local, mesh=mesh, in_specs=in_specs, out_specs=out_specs, check_vma=False)
```

profile of v0, /device:TPU:16, one launch (start us, length us, event | category | flops | bytes accessed | tf_op | source)
XLA Modules:
  0.0 26.4 jit_solution(18191249645007946026)
XLA Ops:
  0.6 3.2 %shard_map.94 = (s32[64,128]{1,0:T(8,128)S(1)}, s32[1,64]{1,0:T(1,128)}, f32[3,64,128]{2,1,0:T(8,128)S(1)}, f32[3,64,128]{2,1,0:T(8,128)S(1)}, f32[64,128]{1,0:T...) custom-call(s32[64,128]{1,0:T(8,128)} %bitcast.10, ...), custom_call_target="tpu_custom_call" | custom-call | tf_op jit(solution)/shard_map/pallas_call | solution.py:315
  3.8 1.6 %collective-permute-start = (f32[9,8,128]{2,1,0:T(8,128)S(1)}, f32[9,8,128]{2,1,0:T(8,128)S(1)}, u32[]{:S(2)}, u32[]{:S(2)}) collective-permute-start(f32[9,8,128]{2,1,0:T(8,128)S(1)} %get-tuple-element.37), channel_id=1, source_target_pairs={{0,2},{2,0},{4,6},{6,4},{8,10},{10,8},{12,14},{14,12},{16,18},{18,... | collective-permute-start | bytes 110600 | tf_op jit(solution)/shard_map/ppermute | solution.py:354
  5.4 3.3 %collective-permute-start.1 = (f32[9,8,128]{2,1,0:T(8,128)S(1)}, f32[9,8,128]{2,1,0:T(8,128)S(1)}, u32[]{:S(2)}, u32[]{:S(2)}) collective-permute-start(f32[9,8,128]{2,1,0:T(8,128)S(1)} %get-tuple-element.38), channel_id=1, source_target_pairs={{0,0},{2,4},{4,2},{6,8},{8,6},{10,12},{12,10},{14,16},{16,14},{18,... | collective-permute-start | bytes 110600 | tf_op jit(solution)/shard_map/ppermute | solution.py:353
  8.6 0.0 collective-permute-done.first
  8.7 4.3 %collective-permute-done.1.second = f32[9,8,128]{2,1,0:T(8,128)S(1)} collective-permute-done((f32[9,8,128]{2,1,0:T(8,128)S(1)}, f32[9,8,128]{2,1,0:T(8,128)S(1)}, u32[]{:S(2)}, u32[]{:S(2)}) %collective-permute-start.1) | collective-permute-done | bytes 36896 | tf_op jit(solution)/shard_map/ppermute | solution.py:353
  13.0 0.1 collective-permute-start.2
  13.1 1.3 %collective-permute-done.2.other = f32[4,6,8,128]{3,2,1,0:T(8,128)S(1)} collective-permute-done((f32[4,6,8,128]{3,2,1,0:T(8,128)S(1)}, f32[4,6,8,128]{3,2,1,0:T(8,128)S(1)}, u32[]{:S(2)}, u32[]{:S(2)}) %collective-permute-start.2) | collective-permute-done | bytes 98336 | tf_op jit(solution)/shard_map/ppermute | solution.py:366
  14.4 2.8 %shard_map.96 = (f32[3,64,128]{2,1,0:T(8,128)S(1)}, f32[3,64,128]{2,1,0:T(8,128)S(1)}, f32[64,128]{1,0:T(8,128)S(1)}, f32[3,64,128]{2,1,0:T(8,128)S(1)}, bf16[64...) custom-call(s32[64,128]{1,0:T(8,128)S(1)} %get-tuple-element.27.cell, ...), custom_call_target="tpu_custom_call" | custom-call | tf_op jit(solution)/shard_map/pallas_call | solution.py:315
  17.2 0.1 collective-permute-start.3
  17.3 3.9 %collective-permute-start.4 = (f32[8,8,128]{2,1,0:T(8,128)S(1)}, f32[8,8,128]{2,1,0:T(8,128)S(1)}, u32[]{:S(2)}, u32[]{:S(2)}) collective-permute-start(f32[8,8,128]{2,1,0:T(8,128)S(1)} %get-tuple-element.47), channel_id=1, source_target_pairs={{0,0},{2,4},{4,2},{6,8},{8,6},{10,12},{12,10},{14,16},{16,14},{18,... | collective-permute-start | bytes 98312 | tf_op jit(solution)/shard_map/ppermute | solution.py:353
  21.1 0.0 collective-permute-done.3.first
  21.2 3.7 %collective-permute-done.4.second = f32[8,8,128]{2,1,0:T(8,128)S(1)} collective-permute-done((f32[8,8,128]{2,1,0:T(8,128)S(1)}, f32[8,8,128]{2,1,0:T(8,128)S(1)}, u32[]{:S(2)}, u32[]{:S(2)}) %collective-permute-start.4) | collective-permute-done | bytes 32800 | tf_op jit(solution)/shard_map/ppermute | solution.py:353
  24.9 1.6 %shard_map.97 = (f32[3,64,128]{2,1,0:T(8,128)}, f32[3,64,128]{2,1,0:T(8,128)}, f32[64,128]{1,0:T(8,128)}) custom-call(f32[3,64,128]{2,1,0:T(8,128)S(1)} %get-tuple-element.39.frac, f32[3,64,128]{2,1,0:T(8,128)S(1)} %get-tuple-element.40.vel, f32[64,128]{1,0:T(8,128)S(1)} %get-tuple-element.41.stress, f32[3,64,128]{2,1,0:T(8,128)S(1)} %get-tuple-element.42.kept, ...), custom_call_target="tpu_custom_call" | custom-call | tf_op jit(solution)/shard_map/pallas_call | solution.py:315
  (1 shorter events, 0.0 us)
Async XLA Ops:
  3.8 4.8 %collective-permute-start = (f32[9,8,128]{2,1,0:T(8,128)S(1)}, f32[9,8,128]{2,1,0:T(8,128)S(1)}, u32[]{:S(2)}, u32[]{:S(2)}) collective-permute-start(f32[9,8,128]{2,1,0:T(8,128)S(1)} %get-tuple-element.37), channel_id=1, source_target_pairs={{0,2},{2,0},{4,6},{6,4},{8,10},{10,8},{12,14},{14,12},{16,18},{18,... | collective-permute-start | bytes 110600 | tf_op jit(solution)/shard_map/ppermute | solution.py:354
  5.4 7.6 %collective-permute-start.1 = (f32[9,8,128]{2,1,0:T(8,128)S(1)}, f32[9,8,128]{2,1,0:T(8,128)S(1)}, u32[]{:S(2)}, u32[]{:S(2)}) collective-permute-start(f32[9,8,128]{2,1,0:T(8,128)S(1)} %get-tuple-element.38), channel_id=1, source_target_pairs={{0,0},{2,4},{4,2},{6,8},{8,6},{10,12},{12,10},{14,16},{16,14},{18,... | collective-permute-start | bytes 110600 | tf_op jit(solution)/shard_map/ppermute | solution.py:353
  13.0 1.4 %collective-permute-start.2 = (f32[4,6,8,128]{3,2,1,0:T(8,128)S(1)}, f32[4,6,8,128]{3,2,1,0:T(8,128)S(1)}, u32[]{:S(2)}, u32[]{:S(2)}) collective-permute-start(f32[4,6,8,128]{3,2,1,0:T(8,128)S(1)} %shard_map.95.fields), channel_id=1, source_target_pairs={{0,1},{1,0},{2,3},{3,2},{4,5},{5,4},{6,7},{7,6},{8,9},{9,8},{10,11... | collective-permute-start | bytes 294920 | tf_op jit(solution)/shard_map/ppermute | solution.py:366
  17.2 4.0 %collective-permute-start.3 = (f32[8,8,128]{2,1,0:T(8,128)S(1)}, f32[8,8,128]{2,1,0:T(8,128)S(1)}, u32[]{:S(2)}, u32[]{:S(2)}) collective-permute-start(f32[8,8,128]{2,1,0:T(8,128)S(1)} %get-tuple-element.46), channel_id=1, source_target_pairs={{0,2},{2,0},{4,6},{6,4},{8,10},{10,8},{12,14},{14,12},{16,18},{18,... | collective-permute-start | bytes 98312 | tf_op jit(solution)/shard_map/ppermute | solution.py:354
  17.3 7.6 %collective-permute-start.4 = (f32[8,8,128]{2,1,0:T(8,128)S(1)}, f32[8,8,128]{2,1,0:T(8,128)S(1)}, u32[]{:S(2)}, u32[]{:S(2)}) collective-permute-start(f32[8,8,128]{2,1,0:T(8,128)S(1)} %get-tuple-element.47), channel_id=1, source_target_pairs={{0,0},{2,4},{4,2},{6,8},{8,6},{10,12},{12,10},{14,16},{16,14},{18,... | collective-permute-start | bytes 98312 | tf_op jit(solution)/shard_map/ppermute | solution.py:353
where the time goes:
time: 26.6 us; the launch traced here: 26.4 us
  waiting for transfers between devices  9.37 us (35%)
  starting transfers between devices  8.83 us (33%)
  Pallas kernels  7.55 us (28%)
  between operations  0.69 us (3%)
    ppermute x2, waiting for transfers between devices, exchange(): second = lax.ppermute(second, 'space', matching(1))  8.05 us
    pallas_call x4, Pallas kernels, call(): pl.pallas_call(kernel, out_shape=[jax.ShapeDtypeStruct(*(s if isinstance(...  7.55 us
    ppermute x2, starting transfers between devices, exchange(): second = lax.ppermute(second, 'space', matching(1))  7.14 us
    ppermute x2, starting transfers between devices, exchange(): first = lax.ppermute(first, 'space', matching(0))  1.63 us
    ppermute x1, waiting for transfers between devices, local(): other = lax.ppermute(fields, 'phase', swap)  1.29 us
  transfers between devices with their start and end apart: 5, of which 3 were waited for; matrix products, arithmetic and copies ran while one was open for 0% of the time, Pallas kernels for 0%

commit v1 on v0

--- a/solution.py
+++ b/solution.py
@@ -79,28 +79,28 @@
     return 4 * q // 8 * 8, (4 * q + 5) // 8 * 8 + 8
 
 
-def side_by_side(ref, rows):
-    return jnp.concatenate([ref[row] for row in rows], axis=1)
-
-
 def block_row(h, b, nbz):
     return b // GROUP * nbz + h * GROUP + b % GROUP
 
 
-def deposit(planes, tiles, factors, right, sums, out, nby, nbz):
+def deposit(planes, tiles, factors, sums, out, nby, nbz):
     sums[...] = jnp.zeros_like(sums)
     blocks = nby * GROUP
 
     def group(h, carry):
+        columns, lines = [], []
         for b in range(blocks):
             row, q = block_row(h, b, nbz), b % GROUP
             get = lambda k: planes[k, pl.ds(row, 8, stride=0), :]
             at = lax.broadcasted_iota(jnp.int32, (8, 128), 0).astype(F32)
             wy = place(at, get(YAT) - 1.0, [get(WY + t) for t in range(3)])
+            pieces = []
             for x in range(0, 6, 2):
                 high, low = halves(jnp.concatenate([get(WX + x) * wy, get(WX + x + 1) * wy], axis=0))
                 tiles[row, 8 * x : 8 * x + 16] = high
                 tiles[row, 48 + 8 * x : 64 + 8 * x] = low
+                pieces.append((high, low))
+            lines.append(jnp.concatenate([p[0] for p in pieces] + [p[1] for p in pieces], axis=0))
             first, last = z_rows(q)
             steps = (last - first) // 8
             get = lambda k: jnp.concatenate([planes[k, pl.ds(row, 8, stride=0), :]] * steps, axis=0)
@@ -115,14 +115,14 @@
             zeros = lambda n: [jnp.zeros((n, 128), F32)] if n else []
             high = [part.astype(BF16).astype(F32) for part in parts]
             low = [part - h for part, h in zip(parts, high)]
-            for at, values in ((0, high), (128, low)):
-                stack = []
+            stack = []
+            for values in (high, low):
                 for value in values:
                     stack += zeros(first) + [value] + zeros(WINDOW - last)
                 stack += zeros(128 - CHANNELS * WINDOW)
-                right[b, at : at + 128] = jnp.concatenate(stack, axis=0).astype(BF16)
-        a = side_by_side(tiles, [block_row(h, b, nbz) for b in range(blocks)])
-        o = lax.dot_general(a, side_by_side(right, range(blocks)), (((1,), (1,)), ((), ())),
+            columns.append(jnp.concatenate(stack, axis=0).astype(BF16))
+        a = jnp.concatenate(lines, axis=1)
+        o = lax.dot_general(a, jnp.concatenate(columns, axis=1), (((1,), (1,)), ((), ())),
                             preferred_element_type=F32)
         o = o[0:48] + o[48:96]
         o = o[:, 0:128] + o[:, 128:256]
@@ -260,7 +260,7 @@
 
 def first_kernel(sizes, *refs):
     sources, inputs, rest = refs[:7], refs[7:14], refs[14:]
-    kept, tiles, factors, dep, first, second, planes, right, sums, sems = rest
+    kept, tiles, factors, dep, first, second, planes, sums, sems = rest
     copies = [pltpu.make_async_copy(a, b, sems.at[k]) for k, (a, b) in enumerate(zip(sources, inputs))]
     for copy in copies:
         copy.start()
@@ -272,7 +272,7 @@
     m = jnp.where(live, mass[...], 0.0)
     s = jnp.where(live, stress[...], 0.0)
     prepare(cell[...], [frac[k] for k in range(3)], planes, kept, m, [vel[k] for k in range(3)], s, *sizes)
-    deposit(planes, tiles, factors, right, sums, dep, *sizes)
+    deposit(planes, tiles, factors, sums, dep, *sizes)
     Side().send(dep, first, second, coef)
 
 
@@ -282,7 +282,7 @@
 
 def middle_kernel(sizes, cell, frac, vel, mass, stress, coef, kept, tiles, factors, fields, other, first, second,
                   new_frac, new_vel, new_stress, new_kept, new_tiles, new_factors, dep, new_first, new_second,
-                  planes, right, sums, turned, sampled):
+                  planes, sums, turned, sampled):
     side = Side()
     own_mass, own_vel = node_velocity(fields)
     other_mass, other_vel = node_velocity(other)
@@ -297,7 +297,7 @@
     m = jnp.where(live, mass[...], 0.0)
     s = jnp.where(live, state[2], 0.0)
     prepare(cell[...], state[0], planes, new_kept, m, state[1], s, *sizes)
-    deposit(planes, new_tiles, new_factors, right, sums, dep, *sizes)
+    deposit(planes, new_tiles, new_factors, sums, dep, *sizes)
     side.send(dep, new_first, new_second)
 
 
@@ -344,7 +344,6 @@
     grid = (4, layers + 2, ny, nz)
     saved = [triple, ((blocks, 96, slots), BF16), (blocks, 2, 16, slots)]
     planes = pltpu.VMEM((PLANES,) + particle, F32)
-    right = pltpu.VMEM((nby * GROUP, 256, slots), BF16)
     sums = pltpu.VMEM((CHANNELS, (layers + 2) * ny, nz), F32)
     turned = pltpu.VMEM((4, nz + 24, 128), F32)
     sampled = pltpu.VMEM((4,) + particle, F32)
@@ -359,7 +358,7 @@
     *loaded, kept, tiles, factors, dep, first, second = call(
         functools.partial(first_kernel, sizes),
         [(a.shape, a.dtype) for a in inputs] + saved + [grid, sent, sent],
-        [planes, right, sums, pltpu.SemaphoreType.DMA((7,))],
+        [planes, sums, pltpu.SemaphoreType.DMA((7,))],
         *[pltpu.with_memory_space_constraint(a, pltpu.HBM) for a in inputs], space=pltpu.HBM)
     first, second = exchange(first, second)
     fields, = call(total_kernel, [grid], [], dep, first, second)
@@ -368,7 +367,7 @@
     frac, vel, stress, kept, tiles, factors, dep, first, second = call(
         functools.partial(middle_kernel, sizes),
         [triple, triple, particle] + saved + [grid, sent, sent],
-        [planes, right, sums, turned, sampled],
+        [planes, sums, turned, sampled],
         loaded[0], *loaded[2:], kept, tiles, factors, fields, other, first, second)
     first, second = exchange(first, second)
     frac, vel, stress = call(

time: 26.6 us -> 25.9 us (0.974)
  Pallas kernels: 7.55 us -> 6.8 us
    pallas_call x4, Pallas kernels: 7.55 us -> 6.8 us  [call(): pl.pallas_call(kernel, out_shape=[jax.ShapeDtypeStruct(*(s if isinstance(...]
where the time goes in v1:
time: 25.9 us; the launch traced here: 25.7 us
  waiting for transfers between devices  9.38 us (36%)
  starting transfers between devices  8.83 us (34%)
  Pallas kernels  6.8 us (26%)
  between operations  0.69 us (3%)
    ppermute x2, waiting for transfers between devices, exchange(): second = lax.ppermute(second, 'space', matching(1))  8.05 us
    ppermute x2, starting transfers between devices, exchange(): second = lax.ppermute(second, 'space', matching(1))  7.13 us
    pallas_call x4, Pallas kernels, call(): pl.pallas_call(kernel, out_shape=[jax.ShapeDtypeStruct(*(s if isinstance(...  6.8 us
    ppermute x2, starting transfers between devices, exchange(): first = lax.ppermute(first, 'space', matching(0))  1.63 us
    ppermute x1, waiting for transfers between devices, local(): other = lax.ppermute(fields, 'phase', swap)  1.29 us
  transfers between devices with their start and end apart: 5, of which 3 were waited for; matrix products, arithmetic and copies ran while one was open for 0% of the time, Pallas kernels for 0%

profile of v1, /device:TPU:16, one launch (start us, length us, event | category | flops | bytes accessed | tf_op | source)
XLA Modules:
  0.0 25.7 jit_solution(11638056699739083438)
XLA Ops:
  0.6 2.7 %shard_map.94 = (s32[64,128]{1,0:T(8,128)S(1)}, s32[1,64]{1,0:T(1,128)}, f32[3,64,128]{2,1,0:T(8,128)S(1)}, f32[3,64,128]{2,1,0:T(8,128)S(1)}, f32[64,128]{1,0:T...) custom-call(s32[64,128]{1,0:T(8,128)} %bitcast.10, ...), custom_call_target="tpu_custom_call" | custom-call | tf_op jit(solution)/shard_map/pallas_call | solution.py:315
  3.4 1.6 %collective-permute-start = (f32[9,8,128]{2,1,0:T(8,128)S(1)}, f32[9,8,128]{2,1,0:T(8,128)S(1)}, u32[]{:S(2)}, u32[]{:S(2)}) collective-permute-start(f32[9,8,128]{2,1,0:T(8,128)S(1)} %get-tuple-element.37), channel_id=1, source_target_pairs={{0,2},{2,0},{4,6},{6,4},{8,10},{10,8},{12,14},{14,12},{16,18},{18,... | collective-permute-start | bytes 110600 | tf_op jit(solution)/shard_map/ppermute | solution.py:353
  4.9 3.3 %collective-permute-start.1 = (f32[9,8,128]{2,1,0:T(8,128)S(1)}, f32[9,8,128]{2,1,0:T(8,128)S(1)}, u32[]{:S(2)}, u32[]{:S(2)}) collective-permute-start(f32[9,8,128]{2,1,0:T(8,128)S(1)} %get-tuple-element.38), channel_id=1, source_target_pairs={{0,0},{2,4},{4,2},{6,8},{8,6},{10,12},{12,10},{14,16},{16,14},{18,... | collective-permute-start | bytes 110600 | tf_op jit(solution)/shard_map/ppermute | solution.py:352
  8.2 0.0 collective-permute-done.first
  8.2 4.3 %collective-permute-done.1.second = f32[9,8,128]{2,1,0:T(8,128)S(1)} collective-permute-done((f32[9,8,128]{2,1,0:T(8,128)S(1)}, f32[9,8,128]{2,1,0:T(8,128)S(1)}, u32[]{:S(2)}, u32[]{:S(2)}) %collective-permute-start.1) | collective-permute-done | bytes 36896 | tf_op jit(solution)/shard_map/ppermute | solution.py:352
  12.6 0.1 collective-permute-start.2
  12.7 1.3 %collective-permute-done.2.other = f32[4,6,8,128]{3,2,1,0:T(8,128)S(1)} collective-permute-done((f32[4,6,8,128]{3,2,1,0:T(8,128)S(1)}, f32[4,6,8,128]{3,2,1,0:T(8,128)S(1)}, u32[]{:S(2)}, u32[]{:S(2)}) %collective-permute-start.2) | collective-permute-done | bytes 98336 | tf_op jit(solution)/shard_map/ppermute | solution.py:365
  14.0 2.5 %shard_map.96 = (f32[3,64,128]{2,1,0:T(8,128)S(1)}, f32[3,64,128]{2,1,0:T(8,128)S(1)}, f32[64,128]{1,0:T(8,128)S(1)}, f32[3,64,128]{2,1,0:T(8,128)S(1)}, bf16[64...) custom-call(s32[64,128]{1,0:T(8,128)S(1)} %get-tuple-element.27.cell, ...), custom_call_target="tpu_custom_call" | custom-call | tf_op jit(solution)/shard_map/pallas_call | solution.py:315
  16.5 0.1 collective-permute-start.3
  16.5 3.9 %collective-permute-start.4 = (f32[8,8,128]{2,1,0:T(8,128)S(1)}, f32[8,8,128]{2,1,0:T(8,128)S(1)}, u32[]{:S(2)}, u32[]{:S(2)}) collective-permute-start(f32[8,8,128]{2,1,0:T(8,128)S(1)} %get-tuple-element.47), channel_id=1, source_target_pairs={{0,0},{2,4},{4,2},{6,8},{8,6},{10,12},{12,10},{14,16},{16,14},{18,... | collective-permute-start | bytes 98312 | tf_op jit(solution)/shard_map/ppermute | solution.py:352
  20.4 0.0 collective-permute-done.3.first
  20.4 3.7 %collective-permute-done.4.second = f32[8,8,128]{2,1,0:T(8,128)S(1)} collective-permute-done((f32[8,8,128]{2,1,0:T(8,128)S(1)}, f32[8,8,128]{2,1,0:T(8,128)S(1)}, u32[]{:S(2)}, u32[]{:S(2)}) %collective-permute-start.4) | collective-permute-done | bytes 32800 | tf_op jit(solution)/shard_map/ppermute | solution.py:352
  24.1 1.6 %shard_map.97 = (f32[3,64,128]{2,1,0:T(8,128)}, f32[3,64,128]{2,1,0:T(8,128)}, f32[64,128]{1,0:T(8,128)}) custom-call(f32[3,64,128]{2,1,0:T(8,128)S(1)} %get-tuple-element.39.frac, f32[3,64,128]{2,1,0:T(8,128)S(1)} %get-tuple-element.40.vel, f32[64,128]{1,0:T(8,128)S(1)} %get-tuple-element.41.stress, f32[3,64,128]{2,1,0:T(8,128)S(1)} %get-tuple-element.42.kept, ...), custom_call_target="tpu_custom_call" | custom-call | tf_op jit(solution)/shard_map/pallas_call | solution.py:315
  (1 shorter events, 0.0 us)
Async XLA Ops:
  3.4 4.8 %collective-permute-start = (f32[9,8,128]{2,1,0:T(8,128)S(1)}, f32[9,8,128]{2,1,0:T(8,128)S(1)}, u32[]{:S(2)}, u32[]{:S(2)}) collective-permute-start(f32[9,8,128]{2,1,0:T(8,128)S(1)} %get-tuple-element.37), channel_id=1, source_target_pairs={{0,2},{2,0},{4,6},{6,4},{8,10},{10,8},{12,14},{14,12},{16,18},{18,... | collective-permute-start | bytes 110600 | tf_op jit(solution)/shard_map/ppermute | solution.py:353
  4.9 7.6 %collective-permute-start.1 = (f32[9,8,128]{2,1,0:T(8,128)S(1)}, f32[9,8,128]{2,1,0:T(8,128)S(1)}, u32[]{:S(2)}, u32[]{:S(2)}) collective-permute-start(f32[9,8,128]{2,1,0:T(8,128)S(1)} %get-tuple-element.38), channel_id=1, source_target_pairs={{0,0},{2,4},{4,2},{6,8},{8,6},{10,12},{12,10},{14,16},{16,14},{18,... | collective-permute-start | bytes 110600 | tf_op jit(solution)/shard_map/ppermute | solution.py:352
  12.6 1.4 %collective-permute-start.2 = (f32[4,6,8,128]{3,2,1,0:T(8,128)S(1)}, f32[4,6,8,128]{3,2,1,0:T(8,128)S(1)}, u32[]{:S(2)}, u32[]{:S(2)}) collective-permute-start(f32[4,6,8,128]{3,2,1,0:T(8,128)S(1)} %shard_map.95.fields), channel_id=1, source_target_pairs={{0,1},{1,0},{2,3},{3,2},{4,5},{5,4},{6,7},{7,6},{8,9},{9,8},{10,11... | collective-permute-start | bytes 294920 | tf_op jit(solution)/shard_map/ppermute | solution.py:365
  16.5 4.0 %collective-permute-start.3 = (f32[8,8,128]{2,1,0:T(8,128)S(1)}, f32[8,8,128]{2,1,0:T(8,128)S(1)}, u32[]{:S(2)}, u32[]{:S(2)}) collective-permute-start(f32[8,8,128]{2,1,0:T(8,128)S(1)} %get-tuple-element.46), channel_id=1, source_target_pairs={{0,2},{2,0},{4,6},{6,4},{8,10},{10,8},{12,14},{14,12},{16,18},{18,... | collective-permute-start | bytes 98312 | tf_op jit(solution)/shard_map/ppermute | solution.py:353
  16.5 7.6 %collective-permute-start.4 = (f32[8,8,128]{2,1,0:T(8,128)S(1)}, f32[8,8,128]{2,1,0:T(8,128)S(1)}, u32[]{:S(2)}, u32[]{:S(2)}) collective-permute-start(f32[8,8,128]{2,1,0:T(8,128)S(1)} %get-tuple-element.47), channel_id=1, source_target_pairs={{0,0},{2,4},{4,2},{6,8},{8,6},{10,12},{12,10},{14,16},{16,14},{18,... | collective-permute-start | bytes 98312 | tf_op jit(solution)/shard_map/ppermute | solution.py:352

commit v2 on v1

--- a/solution.py
+++ b/solution.py
@@ -48,7 +48,7 @@
     return high, (value - high.astype(F32)).astype(BF16)
 
 
-def prepare(cell, frac, planes, kept, mass, vel, stress, nby, nbz):
+def prepare_places(cell, frac, planes, kept, nby, nbz):
     wx, _ = spline(frac[0])
     wy, _ = spline(frac[1])
     wz, dz = spline(frac[2])
@@ -64,13 +64,15 @@
         planes[DZ + t] = dz[t]
     for x in range(6):
         planes[WX + x] = place(float(x), at_x, wx)
-    position = (at_x + (frac[0] - 2.0), at_y + (frac[1] - 2.0 * nby))
-    kept[XC] = position[0]
-    kept[YC] = position[1]
+    kept[XC] = at_x + (frac[0] - 2.0)
+    kept[YC] = at_y + (frac[1] - 2.0 * nby)
+
+
+def prepare_channels(planes, kept, mass, vel, stress):
     scaled = (4.0 * time_step) * stress
     planes[CHANNEL] = mass
-    planes[CHANNEL + 1] = mass * vel[0] - scaled * position[0]
-    planes[CHANNEL + 2] = mass * vel[1] - scaled * position[1]
+    planes[CHANNEL + 1] = mass * vel[0] - scaled * kept[XC]
+    planes[CHANNEL + 2] = mass * vel[1] - scaled * kept[YC]
     planes[CHANNEL + 3] = mass * vel[2]
     planes[CHANNEL + 4] = scaled
 
@@ -144,8 +146,9 @@
     out[3] = mz
 
 
-def gather(vel, tiles, factors, turned, sampled, nby, nbz):
-    blocks = nby * GROUP
+def gather(vel, tiles, factors, turned, sampled, nby, nbz, ready=None):
+    parts = 1 if ready is None else nby
+    blocks = nby // parts * GROUP
     shape = vel[0].shape
     x = lax.broadcasted_iota(jnp.int32, shape, 0).astype(F32) - 2.5
     y = lax.broadcasted_iota(jnp.int32, shape, 1).astype(F32) + (0.5 - 2.0 * nby)
@@ -158,13 +161,13 @@
         turned[c, EDGE : EDGE + 128] = v.T
     pad = jnp.zeros((32, 128), F32).astype(BF16)
 
-    def group(h, carry):
+    def group(h, part):
         at = pl.multiple_of(4 * GROUP * h, 8)
         v = jnp.concatenate([turned[c, pl.ds(at, WINDOW)] for c in range(4)], axis=0).astype(BF16)
-        rows = [block_row(h, b, nbz) for b in range(blocks)]
+        rows = [part * nbz + block_row(h, b, nbz) for b in range(blocks)]
         stack = []
-        for part in (0, 48):
-            piece = jnp.concatenate([tiles[row, part : part + 48] for row in rows], axis=1)
+        for half in (0, 48):
+            piece = jnp.concatenate([tiles[row, half : half + 48] for row in rows], axis=1)
             stack += [piece, piece, jnp.concatenate([pad] * blocks, axis=1)]
         t = jnp.dot(jnp.concatenate([v, v], axis=1), jnp.concatenate(stack, axis=0), preferred_element_type=F32)
         for b, row in enumerate(rows):
@@ -174,9 +177,12 @@
             vz = read(2)
             for c, value in enumerate((w * read(0), w * read(1), w * vz, w * read(3) + d * vz)):
                 sampled[c, pl.ds(row, 1), :] = jnp.sum(value, axis=0, keepdims=True)
-        return carry
-
-    lax.fori_loop(0, nbz // GROUP, group, 0, unroll=True)
+        return part
+
+    for part in range(parts):
+        lax.fori_loop(0, nbz // GROUP, group, part, unroll=True)
+        if ready is not None:
+            ready(pl.ds(part * nbz, nbz))
 
 
 def node_velocity(fields):
@@ -239,40 +245,44 @@
     return lax.broadcasted_iota(jnp.int32, shape, 1).astype(F32) < column
 
 
-def advance(sampled, kept, frac_ref, vel_ref, stress_ref):
-    live = kept[LIVE] > 0.5
-    vel = [sampled[k] for k in range(3)]
-    rate = sampled[3] - kept[XC] * vel[0] - kept[YC] * vel[1]
-    old = stress_ref[...]
+def advance(sampled, kept, frac_ref, vel_ref, stress_ref, rows=slice(None)):
+    live = kept[LIVE, rows] > 0.5
+    vel = [sampled[k, rows] for k in range(3)]
+    rate = sampled[3, rows] - kept[XC, rows] * vel[0] - kept[YC, rows] * vel[1]
+    old = stress_ref[rows]
     stress = jnp.where(live, old - (time_step * bulk_modulus * 4.0) * rate, old)
-    frac = [jnp.where(live, frac_ref[k] + time_step * vel[k], frac_ref[k]) for k in range(3)]
-    vel = [jnp.where(live, vel[k], vel_ref[k]) for k in range(3)]
+    frac = [jnp.where(live, frac_ref[k, rows] + time_step * vel[k], frac_ref[k, rows]) for k in range(3)]
+    vel = [jnp.where(live, vel[k], vel_ref[k, rows]) for k in range(3)]
     return frac, vel, stress
 
 
-def store_state(state, new_frac, new_vel, new_stress):
+def store_state(state, new_frac, new_vel, new_stress, rows=slice(None)):
     frac, vel, stress = state
     for k in range(3):
-        new_frac[k] = frac[k]
-        new_vel[k] = vel[k]
-    new_stress[...] = stress
+        new_frac[k, rows] = frac[k]
+        new_vel[k, rows] = vel[k]
+    new_stress[rows] = stress
 
 
 def first_kernel(sizes, *refs):
     sources, inputs, rest = refs[:7], refs[7:14], refs[14:]
     kept, tiles, factors, dep, first, second, planes, sums, sems = rest
     copies = [pltpu.make_async_copy(a, b, sems.at[k]) for k, (a, b) in enumerate(zip(sources, inputs))]
-    for copy in copies:
-        copy.start()
-    for copy in copies:
-        copy.wait()
     cell, count, frac, vel, mass, stress, coef = inputs
+    for k in (2, 0, 1, 4, 5, 3, 6):
+        copies[k].start()
+    copies[2].wait()
+    copies[0].wait()
+    prepare_places(cell[...], [frac[k] for k in range(3)], planes, kept, *sizes)
+    for k in (1, 4, 5, 3):
+        copies[k].wait()
     live = live_mask(count, cell.shape)
     kept[LIVE] = jnp.where(live, 1.0, 0.0)
     m = jnp.where(live, mass[...], 0.0)
     s = jnp.where(live, stress[...], 0.0)
-    prepare(cell[...], [frac[k] for k in range(3)], planes, kept, m, [vel[k] for k in range(3)], s, *sizes)
+    prepare_channels(planes, kept, m, [vel[k] for k in range(3)], s)
     deposit(planes, tiles, factors, sums, dep, *sizes)
+    copies[6].wait()
     Side().send(dep, first, second, coef)
 
 
@@ -296,30 +306,45 @@
     live = kept[LIVE] > 0.5
     m = jnp.where(live, mass[...], 0.0)
     s = jnp.where(live, state[2], 0.0)
-    prepare(cell[...], state[0], planes, new_kept, m, state[1], s, *sizes)
+    prepare_places(cell[...], state[0], planes, new_kept, *sizes)
+    prepare_channels(planes, new_kept, m, state[1], s)
     deposit(planes, new_tiles, new_factors, sums, dep, *sizes)
     side.send(dep, new_first, new_second)
 
 
 def last_kernel(sizes, frac, vel, stress, kept, tiles, factors, dep, first, second,
-                new_frac, new_vel, new_stress, turned, sampled):
+                frac_out, vel_out, stress_out, new_frac, new_vel, new_stress, turned, sampled, sems):
     side = Side()
+    copies = []
+
+    def ready(rows):
+        store_state(advance(sampled, kept, frac, vel, stress, rows), new_frac, new_vel, new_stress, rows)
+        pairs = (
+            (new_frac.at[:, rows], frac_out.at[:, rows]),
+            (new_vel.at[:, rows], vel_out.at[:, rows]),
+            (new_stress.at[rows], stress_out.at[rows]),
+        )
+        for source, target in pairs:
+            copy = pltpu.make_async_copy(source, target, sems.at[len(copies)])
+            copy.start()
+            copies.append(copy)
+
     _, nodes = node_velocity(side.layers(dep, first, second))
-    gather([side.keep(v) for v in nodes], tiles, factors, turned, sampled, *sizes)
-    store_state(advance(sampled, kept, frac, vel, stress), new_frac, new_vel, new_stress)
-
-
-def call(kernel, outs, scratch, *args, space=pltpu.VMEM, cost=None, limit=24 << 20):
+    gather([side.keep(v) for v in nodes], tiles, factors, turned, sampled, *sizes, ready)
+    for copy in copies:
+        copy.wait()
+
+
+def call(kernel, outs, scratch, *args, space=pltpu.VMEM, out_space=pltpu.VMEM):
     spec = pl.BlockSpec(memory_space=space)
-    vmem = pl.BlockSpec(memory_space=pltpu.VMEM)
+    out_spec = pl.BlockSpec(memory_space=out_space)
     return pl.pallas_call(
         kernel,
         out_shape=[jax.ShapeDtypeStruct(*(s if isinstance(s[0], tuple) else (s, F32))) for s in outs],
         in_specs=[spec] * len(args),
-        out_specs=[vmem] * len(outs),
+        out_specs=[out_spec] * len(outs),
         scratch_shapes=scratch,
-        cost_estimate=cost,
-        compiler_params=pltpu.CompilerParams(vmem_limit_bytes=limit),
+        compiler_params=pltpu.CompilerParams(vmem_limit_bytes=24 << 20),
     )(*args)
 
 
@@ -371,8 +396,10 @@
         loaded[0], *loaded[2:], kept, tiles, factors, fields, other, first, second)
     first, second = exchange(first, second)
     frac, vel, stress = call(
-        functools.partial(last_kernel, sizes), [triple, triple, particle], [turned, sampled],
-        frac, vel, stress, kept, tiles, factors, dep, first, second)
+        functools.partial(last_kernel, sizes), [triple, triple, particle],
+        [pltpu.VMEM(a.shape, F32) for a in (frac, vel, stress)]
+        + [turned, sampled, pltpu.SemaphoreType.DMA((3 * nby,))],
+        frac, vel, stress, kept, tiles, factors, dep, first, second, out_space=pl.ANY)
     return frac[None], vel[None], stress[None]
 
 

time: 25.9 us -> 26.4 us (1.019)
  Pallas kernels: 6.8 us -> 7.33 us
    pallas_call x4, Pallas kernels: 6.8 us -> 7.33 us  [call(): pl.pallas_call(kernel, out_shape=[jax.ShapeDtypeStruct(*(s if isinstance(...]
where the time goes in v2:
time: 26.4 us; the launch traced here: 26.2 us
  waiting for transfers between devices  9.39 us (36%)
  starting transfers between devices  8.82 us (33%)
  Pallas kernels  7.33 us (28%)
  between operations  0.69 us (3%)
    ppermute x2, waiting for transfers between devices, exchange(): second = lax.ppermute(second, 'space', matching(1))  8.05 us
    pallas_call x4, Pallas kernels, call(): pl.pallas_call(kernel, out_shape=[jax.ShapeDtypeStruct(*(s if isinstance(...  7.33 us
    ppermute x2, starting transfers between devices, exchange(): second = lax.ppermute(second, 'space', matching(1))  7.12 us
    ppermute x2, starting transfers between devices, exchange(): first = lax.ppermute(first, 'space', matching(0))  1.63 us
    ppermute x1, waiting for transfers between devices, local(): other = lax.ppermute(fields, 'phase', swap)  1.29 us
  transfers between devices with their start and end apart: 5, of which 3 were waited for; matrix products, arithmetic and copies ran while one was open for 0% of the time, Pallas kernels for 0%

profile of v2, /device:TPU:16, one launch (start us, length us, event | category | flops | bytes accessed | tf_op | source)
XLA Modules:
  0.0 26.2 jit_solution(11054075056526955451)
XLA Ops:
  0.6 3.2 %shard_map.94 = (s32[64,128]{1,0:T(8,128)S(1)}, s32[1,64]{1,0:T(1,128)}, f32[3,64,128]{2,1,0:T(8,128)S(1)}, f32[3,64,128]{2,1,0:T(8,128)S(1)}, f32[64,128]{1,0:T...) custom-call(s32[64,128]{1,0:T(8,128)} %bitcast.10, ...), custom_call_target="tpu_custom_call" | custom-call | tf_op jit(solution)/shard_map/pallas_call | solution.py:341
  3.9 1.6 %collective-permute-start = (f32[9,8,128]{2,1,0:T(8,128)S(1)}, f32[9,8,128]{2,1,0:T(8,128)S(1)}, u32[]{:S(2)}, u32[]{:S(2)}) collective-permute-start(f32[9,8,128]{2,1,0:T(8,128)S(1)} %get-tuple-element.37), channel_id=1, source_target_pairs={{0,2},{2,0},{4,6},{6,4},{8,10},{10,8},{12,14},{14,12},{16,18},{18,... | collective-permute-start | bytes 110600 | tf_op jit(solution)/shard_map/ppermute | solution.py:378
  5.4 3.3 %collective-permute-start.1 = (f32[9,8,128]{2,1,0:T(8,128)S(1)}, f32[9,8,128]{2,1,0:T(8,128)S(1)}, u32[]{:S(2)}, u32[]{:S(2)}) collective-permute-start(f32[9,8,128]{2,1,0:T(8,128)S(1)} %get-tuple-element.38), channel_id=1, source_target_pairs={{0,0},{2,4},{4,2},{6,8},{8,6},{10,12},{12,10},{14,16},{16,14},{18,... | collective-permute-start | bytes 110600 | tf_op jit(solution)/shard_map/ppermute | solution.py:377
  8.7 0.0 collective-permute-done.first
  8.7 4.3 %collective-permute-done.1.second = f32[9,8,128]{2,1,0:T(8,128)S(1)} collective-permute-done((f32[9,8,128]{2,1,0:T(8,128)S(1)}, f32[9,8,128]{2,1,0:T(8,128)S(1)}, u32[]{:S(2)}, u32[]{:S(2)}) %collective-permute-start.1) | collective-permute-done | bytes 36896 | tf_op jit(solution)/shard_map/ppermute | solution.py:377
  13.1 0.1 collective-permute-start.2
  13.2 1.3 %collective-permute-done.2.other = f32[4,6,8,128]{3,2,1,0:T(8,128)S(1)} collective-permute-done((f32[4,6,8,128]{3,2,1,0:T(8,128)S(1)}, f32[4,6,8,128]{3,2,1,0:T(8,128)S(1)}, u32[]{:S(2)}, u32[]{:S(2)}) %collective-permute-start.2) | collective-permute-done | bytes 98336 | tf_op jit(solution)/shard_map/ppermute | solution.py:390
  14.5 2.5 %shard_map.96 = (f32[3,64,128]{2,1,0:T(8,128)S(1)}, f32[3,64,128]{2,1,0:T(8,128)S(1)}, f32[64,128]{1,0:T(8,128)S(1)}, f32[3,64,128]{2,1,0:T(8,128)S(1)}, bf16[64...) custom-call(s32[64,128]{1,0:T(8,128)S(1)} %get-tuple-element.27.cell, ...), custom_call_target="tpu_custom_call" | custom-call | tf_op jit(solution)/shard_map/pallas_call | solution.py:341
  17.0 0.1 collective-permute-start.3
  17.0 3.8 %collective-permute-start.4 = (f32[8,8,128]{2,1,0:T(8,128)S(1)}, f32[8,8,128]{2,1,0:T(8,128)S(1)}, u32[]{:S(2)}, u32[]{:S(2)}) collective-permute-start(f32[8,8,128]{2,1,0:T(8,128)S(1)} %get-tuple-element.47), channel_id=1, source_target_pairs={{0,0},{2,4},{4,2},{6,8},{8,6},{10,12},{12,10},{14,16},{16,14},{18,... | collective-permute-start | bytes 98312 | tf_op jit(solution)/shard_map/ppermute | solution.py:377
  20.9 0.0 collective-permute-done.3.first
  20.9 3.7 %collective-permute-done.4.second = f32[8,8,128]{2,1,0:T(8,128)S(1)} collective-permute-done((f32[8,8,128]{2,1,0:T(8,128)S(1)}, f32[8,8,128]{2,1,0:T(8,128)S(1)}, u32[]{:S(2)}, u32[]{:S(2)}) %collective-permute-start.4) | collective-permute-done | bytes 32800 | tf_op jit(solution)/shard_map/ppermute | solution.py:377
  24.7 1.6 %shard_map.97 = (f32[3,64,128]{2,1,0:T(8,128)}, f32[3,64,128]{2,1,0:T(8,128)}, f32[64,128]{1,0:T(8,128)}) custom-call(f32[3,64,128]{2,1,0:T(8,128)S(1)} %get-tuple-element.39.frac, f32[3,64,128]{2,1,0:T(8,128)S(1)} %get-tuple-element.40.vel, f32[64,128]{1,0:T(8,128)S(1)} %get-tuple-element.41.stress, f32[3,64,128]{2,1,0:T(8,128)S(1)} %get-tuple-element.42.kept, ...), custom_call_target="tpu_custom_call" | custom-call | tf_op jit(solution)/shard_map/pallas_call | solution.py:341
  (1 shorter events, 0.0 us)
Async XLA Ops:
  3.9 4.8 %collective-permute-start = (f32[9,8,128]{2,1,0:T(8,128)S(1)}, f32[9,8,128]{2,1,0:T(8,128)S(1)}, u32[]{:S(2)}, u32[]{:S(2)}) collective-permute-start(f32[9,8,128]{2,1,0:T(8,128)S(1)} %get-tuple-element.37), channel_id=1, source_target_pairs={{0,2},{2,0},{4,6},{6,4},{8,10},{10,8},{12,14},{14,12},{16,18},{18,... | collective-permute-start | bytes 110600 | tf_op jit(solution)/shard_map/ppermute | solution.py:378
  5.4 7.6 %collective-permute-start.1 = (f32[9,8,128]{2,1,0:T(8,128)S(1)}, f32[9,8,128]{2,1,0:T(8,128)S(1)}, u32[]{:S(2)}, u32[]{:S(2)}) collective-permute-start(f32[9,8,128]{2,1,0:T(8,128)S(1)} %get-tuple-element.38), channel_id=1, source_target_pairs={{0,0},{2,4},{4,2},{6,8},{8,6},{10,12},{12,10},{14,16},{16,14},{18,... | collective-permute-start | bytes 110600 | tf_op jit(solution)/shard_map/ppermute | solution.py:377
  13.1 1.4 %collective-permute-start.2 = (f32[4,6,8,128]{3,2,1,0:T(8,128)S(1)}, f32[4,6,8,128]{3,2,1,0:T(8,128)S(1)}, u32[]{:S(2)}, u32[]{:S(2)}) collective-permute-start(f32[4,6,8,128]{3,2,1,0:T(8,128)S(1)} %shard_map.95.fields), channel_id=1, source_target_pairs={{0,1},{1,0},{2,3},{3,2},{4,5},{5,4},{6,7},{7,6},{8,9},{9,8},{10,11... | collective-permute-start | bytes 294920 | tf_op jit(solution)/shard_map/ppermute | solution.py:390
  17.0 4.0 %collective-permute-start.3 = (f32[8,8,128]{2,1,0:T(8,128)S(1)}, f32[8,8,128]{2,1,0:T(8,128)S(1)}, u32[]{:S(2)}, u32[]{:S(2)}) collective-permute-start(f32[8,8,128]{2,1,0:T(8,128)S(1)} %get-tuple-element.46), channel_id=1, source_target_pairs={{0,2},{2,0},{4,6},{6,4},{8,10},{10,8},{12,14},{14,12},{16,18},{18,... | collective-permute-start | bytes 98312 | tf_op jit(solution)/shard_map/ppermute | solution.py:378
  17.0 7.6 %collective-permute-start.4 = (f32[8,8,128]{2,1,0:T(8,128)S(1)}, f32[8,8,128]{2,1,0:T(8,128)S(1)}, u32[]{:S(2)}, u32[]{:S(2)}) collective-permute-start(f32[8,8,128]{2,1,0:T(8,128)S(1)} %get-tuple-element.47), channel_id=1, source_target_pairs={{0,0},{2,4},{4,2},{6,8},{8,6},{10,12},{12,10},{14,16},{16,14},{18,... | collective-permute-start | bytes 98312 | tf_op jit(solution)/shard_map/ppermute | solution.py:377

commit v3 on v1

--- a/solution.py
+++ b/solution.py
@@ -261,7 +261,11 @@
 def first_kernel(sizes, *refs):
     sources, inputs, rest = refs[:7], refs[7:14], refs[14:]
     kept, tiles, factors, dep, first, second, planes, sums, sems = rest
-    copies = [pltpu.make_async_copy(a, b, sems.at[k]) for k, (a, b) in enumerate(zip(sources, inputs))]
+    pairs = []
+    for a, b in zip(sources, inputs):
+        split = len(a.shape) == 3
+        pairs += [(a.at[k], b.at[k]) for k in range(a.shape[0])] if split else [(a, b)]
+    copies = [pltpu.make_async_copy(a, b, sems.at[k]) for k, (a, b) in enumerate(pairs)]
     for copy in copies:
         copy.start()
     for copy in copies:
@@ -358,7 +362,7 @@
     *loaded, kept, tiles, factors, dep, first, second = call(
         functools.partial(first_kernel, sizes),
         [(a.shape, a.dtype) for a in inputs] + saved + [grid, sent, sent],
-        [planes, sums, pltpu.SemaphoreType.DMA((7,))],
+        [planes, sums, pltpu.SemaphoreType.DMA((10 + layers,))],
         *[pltpu.with_memory_space_constraint(a, pltpu.HBM) for a in inputs], space=pltpu.HBM)
     first, second = exchange(first, second)
     fields, = call(total_kernel, [grid], [], dep, first, second)

time: 25.9 us -> 25.9 us (level)
  no operation moved by 1% of the time
where the time goes in v3:
time: 25.9 us; the launch traced here: 25.7 us
  waiting for transfers between devices  9.39 us (36%)
  starting transfers between devices  8.82 us (34%)
  Pallas kernels  6.81 us (26%)
  between operations  0.69 us (3%)
    ppermute x2, waiting for transfers between devices, exchange(): second = lax.ppermute(second, 'space', matching(1))  8.05 us
    ppermute x2, starting transfers between devices, exchange(): second = lax.ppermute(second, 'space', matching(1))  7.12 us
    pallas_call x4, Pallas kernels, call(): pl.pallas_call(kernel, out_shape=[jax.ShapeDtypeStruct(*(s if isinstance(...  6.81 us
    ppermute x2, starting transfers between devices, exchange(): first = lax.ppermute(first, 'space', matching(0))  1.62 us
    ppermute x1, waiting for transfers between devices, local(): other = lax.ppermute(fields, 'phase', swap)  1.29 us
  transfers between devices with their start and end apart: 5, of which 3 were waited for; matrix products, arithmetic and copies ran while one was open for 0% of the time, Pallas kernels for 0%

profile of v3, /device:TPU:16, one launch (start us, length us, event | category | flops | bytes accessed | tf_op | source)
XLA Modules:
  0.0 25.7 jit_solution(5347039662578385247)
XLA Ops:
  0.6 2.7 %shard_map.94 = (s32[64,128]{1,0:T(8,128)S(1)}, s32[1,64]{1,0:T(1,128)}, f32[3,64,128]{2,1,0:T(8,128)S(1)}, f32[3,64,128]{2,1,0:T(8,128)S(1)}, f32[64,128]{1,0:T...) custom-call(s32[64,128]{1,0:T(8,128)} %bitcast.10, ...), custom_call_target="tpu_custom_call" | custom-call | tf_op jit(solution)/shard_map/pallas_call | solution.py:319
  3.4 1.6 %collective-permute-start = (f32[9,8,128]{2,1,0:T(8,128)S(1)}, f32[9,8,128]{2,1,0:T(8,128)S(1)}, u32[]{:S(2)}, u32[]{:S(2)}) collective-permute-start(f32[9,8,128]{2,1,0:T(8,128)S(1)} %get-tuple-element.37), channel_id=1, source_target_pairs={{0,2},{2,0},{4,6},{6,4},{8,10},{10,8},{12,14},{14,12},{16,18},{18,... | collective-permute-start | bytes 110600 | tf_op jit(solution)/shard_map/ppermute | solution.py:357
  4.9 3.3 %collective-permute-start.1 = (f32[9,8,128]{2,1,0:T(8,128)S(1)}, f32[9,8,128]{2,1,0:T(8,128)S(1)}, u32[]{:S(2)}, u32[]{:S(2)}) collective-permute-start(f32[9,8,128]{2,1,0:T(8,128)S(1)} %get-tuple-element.38), channel_id=1, source_target_pairs={{0,0},{2,4},{4,2},{6,8},{8,6},{10,12},{12,10},{14,16},{16,14},{18,... | collective-permute-start | bytes 110600 | tf_op jit(solution)/shard_map/ppermute | solution.py:356
  8.2 0.0 collective-permute-done.first
  8.2 4.3 %collective-permute-done.1.second = f32[9,8,128]{2,1,0:T(8,128)S(1)} collective-permute-done((f32[9,8,128]{2,1,0:T(8,128)S(1)}, f32[9,8,128]{2,1,0:T(8,128)S(1)}, u32[]{:S(2)}, u32[]{:S(2)}) %collective-permute-start.1) | collective-permute-done | bytes 36896 | tf_op jit(solution)/shard_map/ppermute | solution.py:356
  12.6 0.1 collective-permute-start.2
  12.7 1.3 %collective-permute-done.2.other = f32[4,6,8,128]{3,2,1,0:T(8,128)S(1)} collective-permute-done((f32[4,6,8,128]{3,2,1,0:T(8,128)S(1)}, f32[4,6,8,128]{3,2,1,0:T(8,128)S(1)}, u32[]{:S(2)}, u32[]{:S(2)}) %collective-permute-start.2) | collective-permute-done | bytes 98336 | tf_op jit(solution)/shard_map/ppermute | solution.py:369
  14.0 2.5 %shard_map.96 = (f32[3,64,128]{2,1,0:T(8,128)S(1)}, f32[3,64,128]{2,1,0:T(8,128)S(1)}, f32[64,128]{1,0:T(8,128)S(1)}, f32[3,64,128]{2,1,0:T(8,128)S(1)}, bf16[64...) custom-call(s32[64,128]{1,0:T(8,128)S(1)} %get-tuple-element.27.cell, ...), custom_call_target="tpu_custom_call" | custom-call | tf_op jit(solution)/shard_map/pallas_call | solution.py:319
  16.5 0.1 collective-permute-start.3
  16.5 3.8 %collective-permute-start.4 = (f32[8,8,128]{2,1,0:T(8,128)S(1)}, f32[8,8,128]{2,1,0:T(8,128)S(1)}, u32[]{:S(2)}, u32[]{:S(2)}) collective-permute-start(f32[8,8,128]{2,1,0:T(8,128)S(1)} %get-tuple-element.47), channel_id=1, source_target_pairs={{0,0},{2,4},{4,2},{6,8},{8,6},{10,12},{12,10},{14,16},{16,14},{18,... | collective-permute-start | bytes 98312 | tf_op jit(solution)/shard_map/ppermute | solution.py:356
  20.4 0.0 collective-permute-done.3.first
  20.4 3.7 %collective-permute-done.4.second = f32[8,8,128]{2,1,0:T(8,128)S(1)} collective-permute-done((f32[8,8,128]{2,1,0:T(8,128)S(1)}, f32[8,8,128]{2,1,0:T(8,128)S(1)}, u32[]{:S(2)}, u32[]{:S(2)}) %collective-permute-start.4) | collective-permute-done | bytes 32800 | tf_op jit(solution)/shard_map/ppermute | solution.py:356
  24.1 1.6 %shard_map.97 = (f32[3,64,128]{2,1,0:T(8,128)}, f32[3,64,128]{2,1,0:T(8,128)}, f32[64,128]{1,0:T(8,128)}) custom-call(f32[3,64,128]{2,1,0:T(8,128)S(1)} %get-tuple-element.39.frac, f32[3,64,128]{2,1,0:T(8,128)S(1)} %get-tuple-element.40.vel, f32[64,128]{1,0:T(8,128)S(1)} %get-tuple-element.41.stress, f32[3,64,128]{2,1,0:T(8,128)S(1)} %get-tuple-element.42.kept, ...), custom_call_target="tpu_custom_call" | custom-call | tf_op jit(solution)/shard_map/pallas_call | solution.py:319
  (1 shorter events, 0.0 us)
Async XLA Ops:
  3.4 4.8 %collective-permute-start = (f32[9,8,128]{2,1,0:T(8,128)S(1)}, f32[9,8,128]{2,1,0:T(8,128)S(1)}, u32[]{:S(2)}, u32[]{:S(2)}) collective-permute-start(f32[9,8,128]{2,1,0:T(8,128)S(1)} %get-tuple-element.37), channel_id=1, source_target_pairs={{0,2},{2,0},{4,6},{6,4},{8,10},{10,8},{12,14},{14,12},{16,18},{18,... | collective-permute-start | bytes 110600 | tf_op jit(solution)/shard_map/ppermute | solution.py:357
  4.9 7.6 %collective-permute-start.1 = (f32[9,8,128]{2,1,0:T(8,128)S(1)}, f32[9,8,128]{2,1,0:T(8,128)S(1)}, u32[]{:S(2)}, u32[]{:S(2)}) collective-permute-start(f32[9,8,128]{2,1,0:T(8,128)S(1)} %get-tuple-element.38), channel_id=1, source_target_pairs={{0,0},{2,4},{4,2},{6,8},{8,6},{10,12},{12,10},{14,16},{16,14},{18,... | collective-permute-start | bytes 110600 | tf_op jit(solution)/shard_map/ppermute | solution.py:356
  12.6 1.4 %collective-permute-start.2 = (f32[4,6,8,128]{3,2,1,0:T(8,128)S(1)}, f32[4,6,8,128]{3,2,1,0:T(8,128)S(1)}, u32[]{:S(2)}, u32[]{:S(2)}) collective-permute-start(f32[4,6,8,128]{3,2,1,0:T(8,128)S(1)} %shard_map.95.fields), channel_id=1, source_target_pairs={{0,1},{1,0},{2,3},{3,2},{4,5},{5,4},{6,7},{7,6},{8,9},{9,8},{10,11... | collective-permute-start | bytes 294920 | tf_op jit(solution)/shard_map/ppermute | solution.py:369
  16.5 4.0 %collective-permute-start.3 = (f32[8,8,128]{2,1,0:T(8,128)S(1)}, f32[8,8,128]{2,1,0:T(8,128)S(1)}, u32[]{:S(2)}, u32[]{:S(2)}) collective-permute-start(f32[8,8,128]{2,1,0:T(8,128)S(1)} %get-tuple-element.46), channel_id=1, source_target_pairs={{0,2},{2,0},{4,6},{6,4},{8,10},{10,8},{12,14},{14,12},{16,18},{18,... | collective-permute-start | bytes 98312 | tf_op jit(solution)/shard_map/ppermute | solution.py:357
  16.5 7.6 %collective-permute-start.4 = (f32[8,8,128]{2,1,0:T(8,128)S(1)}, f32[8,8,128]{2,1,0:T(8,128)S(1)}, u32[]{:S(2)}, u32[]{:S(2)}) collective-permute-start(f32[8,8,128]{2,1,0:T(8,128)S(1)} %get-tuple-element.47), channel_id=1, source_target_pairs={{0,0},{2,4},{4,2},{6,8},{8,6},{10,12},{12,10},{14,16},{16,14},{18,... | collective-permute-start | bytes 98312 | tf_op jit(solution)/shard_map/ppermute | solution.py:356

commit v4 on v1

--- a/solution.py
+++ b/solution.py
@@ -62,8 +62,12 @@
         planes[WY + t] = wy[t]
         planes[WZ + t] = wz[t]
         planes[DZ + t] = dz[t]
+    here = [at_x == float(k) for k in range(4)]
     for x in range(6):
-        planes[WX + x] = place(float(x), at_x, wx)
+        w = jnp.zeros_like(at_x)
+        for k in range(max(0, x - 2), min(4, x + 1)):
+            w = jnp.where(here[k], wx[x - k], w)
+        planes[WX + x] = w
     position = (at_x + (frac[0] - 2.0), at_y + (frac[1] - 2.0 * nby))
     kept[XC] = position[0]
     kept[YC] = position[1]

time: 25.9 us -> 25.9 us (level)
  no operation moved by 1% of the time
where the time goes in v4:
time: 25.9 us; the launch traced here: 25.7 us
  waiting for transfers between devices  9.39 us (36%)
  starting transfers between devices  8.82 us (34%)
  Pallas kernels  6.81 us (26%)
  between operations  0.69 us (3%)
    ppermute x2, waiting for transfers between devices, exchange(): second = lax.ppermute(second, 'space', matching(1))  8.05 us
    ppermute x2, starting transfers between devices, exchange(): second = lax.ppermute(second, 'space', matching(1))  7.12 us
    pallas_call x4, Pallas kernels, call(): pl.pallas_call(kernel, out_shape=[jax.ShapeDtypeStruct(*(s if isinstance(...  6.81 us
    ppermute x2, starting transfers between devices, exchange(): first = lax.ppermute(first, 'space', matching(0))  1.62 us
    ppermute x1, waiting for transfers between devices, local(): other = lax.ppermute(fields, 'phase', swap)  1.29 us
  transfers between devices with their start and end apart: 5, of which 3 were waited for; matrix products, arithmetic and copies ran while one was open for 0% of the time, Pallas kernels for 0%

profile of v4, /device:TPU:16, one launch (start us, length us, event | category | flops | bytes accessed | tf_op | source)
XLA Modules:
  0.0 25.7 jit_solution(12983281368124067797)
XLA Ops:
  0.6 2.7 %shard_map.94 = (s32[64,128]{1,0:T(8,128)S(1)}, s32[1,64]{1,0:T(1,128)}, f32[3,64,128]{2,1,0:T(8,128)S(1)}, f32[3,64,128]{2,1,0:T(8,128)S(1)}, f32[64,128]{1,0:T...) custom-call(s32[64,128]{1,0:T(8,128)} %bitcast.10, ...), custom_call_target="tpu_custom_call" | custom-call | tf_op jit(solution)/shard_map/pallas_call | solution.py:319
  3.4 1.6 %collective-permute-start = (f32[9,8,128]{2,1,0:T(8,128)S(1)}, f32[9,8,128]{2,1,0:T(8,128)S(1)}, u32[]{:S(2)}, u32[]{:S(2)}) collective-permute-start(f32[9,8,128]{2,1,0:T(8,128)S(1)} %get-tuple-element.37), channel_id=1, source_target_pairs={{0,2},{2,0},{4,6},{6,4},{8,10},{10,8},{12,14},{14,12},{16,18},{18,... | collective-permute-start | bytes 110600 | tf_op jit(solution)/shard_map/ppermute | solution.py:357
  4.9 3.3 %collective-permute-start.1 = (f32[9,8,128]{2,1,0:T(8,128)S(1)}, f32[9,8,128]{2,1,0:T(8,128)S(1)}, u32[]{:S(2)}, u32[]{:S(2)}) collective-permute-start(f32[9,8,128]{2,1,0:T(8,128)S(1)} %get-tuple-element.38), channel_id=1, source_target_pairs={{0,0},{2,4},{4,2},{6,8},{8,6},{10,12},{12,10},{14,16},{16,14},{18,... | collective-permute-start | bytes 110600 | tf_op jit(solution)/shard_map/ppermute | solution.py:356
  8.2 0.0 collective-permute-done.first
  8.2 4.3 %collective-permute-done.1.second = f32[9,8,128]{2,1,0:T(8,128)S(1)} collective-permute-done((f32[9,8,128]{2,1,0:T(8,128)S(1)}, f32[9,8,128]{2,1,0:T(8,128)S(1)}, u32[]{:S(2)}, u32[]{:S(2)}) %collective-permute-start.1) | collective-permute-done | bytes 36896 | tf_op jit(solution)/shard_map/ppermute | solution.py:356
  12.6 0.1 collective-permute-start.2
  12.7 1.3 %collective-permute-done.2.other = f32[4,6,8,128]{3,2,1,0:T(8,128)S(1)} collective-permute-done((f32[4,6,8,128]{3,2,1,0:T(8,128)S(1)}, f32[4,6,8,128]{3,2,1,0:T(8,128)S(1)}, u32[]{:S(2)}, u32[]{:S(2)}) %collective-permute-start.2) | collective-permute-done | bytes 98336 | tf_op jit(solution)/shard_map/ppermute | solution.py:369
  14.0 2.5 %shard_map.96 = (f32[3,64,128]{2,1,0:T(8,128)S(1)}, f32[3,64,128]{2,1,0:T(8,128)S(1)}, f32[64,128]{1,0:T(8,128)S(1)}, f32[3,64,128]{2,1,0:T(8,128)S(1)}, bf16[64...) custom-call(s32[64,128]{1,0:T(8,128)S(1)} %get-tuple-element.27.cell, ...), custom_call_target="tpu_custom_call" | custom-call | tf_op jit(solution)/shard_map/pallas_call | solution.py:319
  16.5 0.1 collective-permute-start.3
  16.5 3.8 %collective-permute-start.4 = (f32[8,8,128]{2,1,0:T(8,128)S(1)}, f32[8,8,128]{2,1,0:T(8,128)S(1)}, u32[]{:S(2)}, u32[]{:S(2)}) collective-permute-start(f32[8,8,128]{2,1,0:T(8,128)S(1)} %get-tuple-element.47), channel_id=1, source_target_pairs={{0,0},{2,4},{4,2},{6,8},{8,6},{10,12},{12,10},{14,16},{16,14},{18,... | collective-permute-start | bytes 98312 | tf_op jit(solution)/shard_map/ppermute | solution.py:356
  20.4 0.0 collective-permute-done.3.first
  20.4 3.7 %collective-permute-done.4.second = f32[8,8,128]{2,1,0:T(8,128)S(1)} collective-permute-done((f32[8,8,128]{2,1,0:T(8,128)S(1)}, f32[8,8,128]{2,1,0:T(8,128)S(1)}, u32[]{:S(2)}, u32[]{:S(2)}) %collective-permute-start.4) | collective-permute-done | bytes 32800 | tf_op jit(solution)/shard_map/ppermute | solution.py:356
  24.1 1.6 %shard_map.97 = (f32[3,64,128]{2,1,0:T(8,128)}, f32[3,64,128]{2,1,0:T(8,128)}, f32[64,128]{1,0:T(8,128)}) custom-call(f32[3,64,128]{2,1,0:T(8,128)S(1)} %get-tuple-element.39.frac, f32[3,64,128]{2,1,0:T(8,128)S(1)} %get-tuple-element.40.vel, f32[64,128]{1,0:T(8,128)S(1)} %get-tuple-element.41.stress, f32[3,64,128]{2,1,0:T(8,128)S(1)} %get-tuple-element.42.kept, ...), custom_call_target="tpu_custom_call" | custom-call | tf_op jit(solution)/shard_map/pallas_call | solution.py:319
  (1 shorter events, 0.0 us)
Async XLA Ops:
  3.4 4.8 %collective-permute-start = (f32[9,8,128]{2,1,0:T(8,128)S(1)}, f32[9,8,128]{2,1,0:T(8,128)S(1)}, u32[]{:S(2)}, u32[]{:S(2)}) collective-permute-start(f32[9,8,128]{2,1,0:T(8,128)S(1)} %get-tuple-element.37), channel_id=1, source_target_pairs={{0,2},{2,0},{4,6},{6,4},{8,10},{10,8},{12,14},{14,12},{16,18},{18,... | collective-permute-start | bytes 110600 | tf_op jit(solution)/shard_map/ppermute | solution.py:357
  4.9 7.6 %collective-permute-start.1 = (f32[9,8,128]{2,1,0:T(8,128)S(1)}, f32[9,8,128]{2,1,0:T(8,128)S(1)}, u32[]{:S(2)}, u32[]{:S(2)}) collective-permute-start(f32[9,8,128]{2,1,0:T(8,128)S(1)} %get-tuple-element.38), channel_id=1, source_target_pairs={{0,0},{2,4},{4,2},{6,8},{8,6},{10,12},{12,10},{14,16},{16,14},{18,... | collective-permute-start | bytes 110600 | tf_op jit(solution)/shard_map/ppermute | solution.py:356
  12.6 1.4 %collective-permute-start.2 = (f32[4,6,8,128]{3,2,1,0:T(8,128)S(1)}, f32[4,6,8,128]{3,2,1,0:T(8,128)S(1)}, u32[]{:S(2)}, u32[]{:S(2)}) collective-permute-start(f32[4,6,8,128]{3,2,1,0:T(8,128)S(1)} %shard_map.95.fields), channel_id=1, source_target_pairs={{0,1},{1,0},{2,3},{3,2},{4,5},{5,4},{6,7},{7,6},{8,9},{9,8},{10,11... | collective-permute-start | bytes 294920 | tf_op jit(solution)/shard_map/ppermute | solution.py:369
  16.5 4.0 %collective-permute-start.3 = (f32[8,8,128]{2,1,0:T(8,128)S(1)}, f32[8,8,128]{2,1,0:T(8,128)S(1)}, u32[]{:S(2)}, u32[]{:S(2)}) collective-permute-start(f32[8,8,128]{2,1,0:T(8,128)S(1)} %get-tuple-element.46), channel_id=1, source_target_pairs={{0,2},{2,0},{4,6},{6,4},{8,10},{10,8},{12,14},{14,12},{16,18},{18,... | collective-permute-start | bytes 98312 | tf_op jit(solution)/shard_map/ppermute | solution.py:357
  16.5 7.6 %collective-permute-start.4 = (f32[8,8,128]{2,1,0:T(8,128)S(1)}, f32[8,8,128]{2,1,0:T(8,128)S(1)}, u32[]{:S(2)}, u32[]{:S(2)}) collective-permute-start(f32[8,8,128]{2,1,0:T(8,128)S(1)} %get-tuple-element.47), channel_id=1, source_target_pairs={{0,0},{2,4},{4,2},{6,8},{8,6},{10,12},{12,10},{14,16},{16,14},{18,... | collective-permute-start | bytes 98312 | tf_op jit(solution)/shard_map/ppermute | solution.py:356
